TPU v7x, 256 devices: a whole 4x4x8 slice. The times are simulated.
256 devices in a mesh: rep: 4 (over z_hi), fsdp: 64 (over y, z_lo, x, core).
Axes of the slice: x: 4, y: 4, z: 8 (z_hi: 4, z_lo: 2; z = z_hi * 2 + z_lo), core: 2. Of those that a mesh axis runs over, the one named last changes fastest.
Arguments:
- activations: bfloat16 [49152, 8192], P(('rep', 'fsdp')), may hold values from -6 to 6
- cotangent: bfloat16 [49152, 14336], P(('rep', 'fsdp')), may hold values from -0.109375 to 0.109375
- projector: bfloat16 [8192, 256], P('fsdp'), may hold values from -0.0625 to 0.0625
- moment1: float32 [256, 14336], P(None, 'fsdp'), may hold values from -4 to 4
- moment2: float32 [256, 14336], P(None, 'fsdp'), may hold values from 0.1 to 4
Outputs:
- moment1_new: float32 [256, 14336], P(None, 'fsdp')
- moment2_new: float32 [256, 14336], P(None, 'fsdp')
- update: bfloat16 [8192, 14336], P(None, 'fsdp')
All inputs are finite; a program needn't handle non-finite values.
Results may differ from a plain program's by a relative error of at most 0.0051.
Values may be sent and summed in bfloat16 or wider, within the bound.
A program may use at most 128 MiB of HBM per device.

v0:
```python
import jax
import jax.numpy as jnp
from jax import lax
from jax.sharding import PartitionSpec as P

STEP = 100


def adam_moments(grad, moment1, moment2):
    return (0.9 * moment1 + 0.1 * grad, 0.999 * moment2 + 0.001 * grad * grad)


def body(activations, cotangent, projector, moment1, moment2):
    low = jnp.dot(
        activations,
        lax.all_gather(projector, "fsdp", axis=0, tiled=True),
        preferred_element_type=jnp.float32,
    ).astype(jnp.bfloat16)
    group_grad = lax.psum_scatter(
        lax.dot_general(
            cotangent, low, (((0,), (0,)), ((), ())), preferred_element_type=jnp.float32
        ),
        "fsdp",
        scatter_dimension=0,
        tiled=True,
    ).T
    grad = lax.psum(group_grad, "rep")
    moment1_new, moment2_new = adam_moments(grad, moment1, moment2)
    first_fix = 1.0 - 0.9**STEP
    second_fix = 1.0 - 0.999**STEP
    direction = (moment1_new / first_fix / (jnp.sqrt(moment2_new / second_fix) + 1e-08)).astype(
        jnp.bfloat16
    )
    update = jnp.dot(
        lax.all_gather(projector, "fsdp", axis=0, tiled=True),
        direction,
        preferred_element_type=jnp.float32,
    )
    return (moment1_new, moment2_new, update.astype(jnp.bfloat16))


def solution(mesh):
    return jax.shard_map(
        body,
        mesh=mesh,
        in_specs=(
            P(("rep", "fsdp"), None),
            P(("rep", "fsdp"), None),
            P("fsdp", None),
            P(None, "fsdp"),
            P(None, "fsdp"),
        ),
        out_specs=(P(None, "fsdp"), P(None, "fsdp"), P(None, "fsdp")),
        check_vma=False,
    )
```

profile of v0, /device:TPU:2, one launch (start us, length us, event | category | flops | bytes accessed | tf_op | source)
XLA Modules:
  0.0 528.2 jit_solution(4577761439493059855)
XLA Ops:
  7.2 0.0 copy-start
  7.2 0.0 all-gather.2.cloned.1.call-start
  7.2 0.7 all-gather.2.cloned.1.call-update
  7.9 0.0 reduce-scatter.4.cloned.1.call-start
  8.0 111.9 %all-gather.2.cloned.1.call-done = bf16[8192,256]{1,0:T(8,128)(2,1)} async-done(((bf16[128,256]{1,0:T(8,128)(2,1)}), bf16[8192,256]{1,0:T(8,128)(2,1)}) %all-gather.2.cloned.1.call-update) | async-done | bytes 4194320 | tf_op jit(solution)/shard_map/all_gather | solution.py:16
  119.8 0.0 copy-done
  119.8 13.7 %convolution_bitcast_fusion = f32[14336,256]{0,1:T(8,128)} fusion(bf16[192,14336]{1,0:T(8,128)(2,1)} %param.6, bf16[192,8192]{1,0:T(8,128)(2,1)S(1)} %copy-done, bf16[8192,256]{1,0:T(8,128)(2,1)} %all-gather.2.cloned.1.call-done), kind=kOutput, calls=%fused_computation | convolution fusion | flops 2214641664 | bytes 27525120 | tf_op jit(solution)/shard_map/dot_general | solution.py:20
  133.5 15.2 %copy.16 = f32[14336,256]{1,0:T(8,128)} copy(f32[14336,256]{0,1:T(8,128)} %convolution_bitcast_fusion) | data formatting | bytes 29360128
  148.7 0.0 copy-start.1
  148.7 0.0 reduce-scatter.4.cloned.1.call-update
  148.7 0.0 all-reduce.2.cloned.1.call-start
  148.7 306.7 %reduce-scatter.4.cloned.1.call-done = f32[224,256]{1,0:T(8,128)} async-done(((f32[14336,256]{1,0:T(8,128)}), f32[224,256]{1,0:T(8,128)}) %reduce-scatter.4.cloned.1.call-update) | async-done | bytes 229392
  455.4 1.8 copy.17
  457.2 0.0 all-reduce.2.cloned.1.call-update
  457.2 0.0 copy-done.1
  457.2 0.8 copy.12
  458.1 1.8 copy.13
  459.9 51.7 %all-reduce.2.cloned.1.call-done = f32[256,224]{1,0:T(8,128)} async-done(((f32[256,224]{1,0:T(8,128)}), f32[256,224]{1,0:T(8,128)}) %all-reduce.2.cloned.1.call-update) | async-done | bytes 229392 | tf_op jit(solution)/shard_map/psum | solution.py:27
  511.5 1.9 fusion.1
  513.4 1.8 copy.14
  515.2 0.8 copy.15
  516.0 5.6 %fusion = bf16[8192,224]{0,1:T(8,128)(2,1)} fusion(bf16[8192,256]{1,0:T(8,128)(2,1)} %all-gather.2.cloned.1.call-done, f32[256,224]{1,0:T(8,128)S(1)} %get-tuple-element.9, f32[256,224]{1,0:T(8,128)} %get-tuple-element.10), kind=kOutput, calls=%fused_computation.2 | convolution fusion | flops 941645824 | bytes 8323072 | tf_op jit(solution)/shard_map/dot_general | solution.py:34
Async XLA Ops:
  7.2 112.7 %copy-start = (bf16[192,8192]{1,0:T(8,128)(2,1)S(1)}, bf16[192,8192]{1,0:T(8,128)(2,1)}, u32[]{:S(2)}) copy-start(bf16[192,8192]{1,0:T(8,128)(2,1)} %param.5) | copy-start | bytes 9437188
  7.2 112.6 %all-gather.2.cloned.1.call-start = ((), (), s32[]{:S(2)}) async-start(), calls=%async_computation.1 | async-start | bytes 4259840 | tf_op jit(solution)/shard_map/all_gather | solution.py:16
  7.9 447.5 %reduce-scatter.4.cloned.1.call-start = ((), (), s32[]{:S(2)}) async-start(), calls=%async_computation.3 | async-start | bytes 14909440
  148.7 308.6 %copy-start.1 = (f32[256,224]{0,1:T(8,128)S(1)}, f32[256,224]{0,1:T(8,128)}, u32[]{:S(2)}) copy-start(f32[256,224]{0,1:T(8,128)} %param.8) | copy-start | bytes 688132
  148.7 362.8 %all-reduce.2.cloned.1.call-start = ((), (), s32[]{:S(2)}) async-start(), calls=%async_computation.2 | async-start | bytes 524288 | tf_op jit(solution)/shard_map/psum | solution.py:27
Sparse Core Ops, SparseCore 0:
  9.8 109.9 all-gather.1
  148.8 306.5 reduce-scatter.3
  458.6 52.8 all-reduce.1
where the time goes:
time: 529 us; the launch traced here: 528 us
  waiting for transfers between devices  471 us (89%)
  local copies, waits for them, and re-layouts  22.1 us (4%)
  matrix products  19.3 us (4%)
  between operations  13.8 us (3%)
    unnamed x4, waiting for transfers between devices  307 us
    all_gather x1, waiting for transfers between devices, body(): lax.all_gather(projector, 'fsdp', axis=0, tiled=True)  112 us
    psum x1, waiting for transfers between devices, body(): grad = lax.psum(group_grad, 'rep')  51.7 us
    unnamed x10, local copies, waits for them, and re-layouts  22.1 us
    dot_general x1, matrix products, body(): lax.dot_general(cotangent, low, (((0,), (0,)), ((), ())), preferred_eleme...  13.7 us
  transfers between devices with their start and end apart: 3, of which 3 were waited for; matrix products, arithmetic and copies ran while one was open for 0% of the time, Pallas kernels for 0%

commit v1 on v0

--- a/solution.py
+++ b/solution.py
@@ -24,7 +24,7 @@
         scatter_dimension=0,
         tiled=True,
     ).T
-    grad = lax.psum(group_grad, "rep")
+    grad = lax.all_gather(group_grad, "rep").sum(axis=0)
     moment1_new, moment2_new = adam_moments(grad, moment1, moment2)
     first_fix = 1.0 - 0.9**STEP
     second_fix = 1.0 - 0.999**STEP

time: 529 us -> 506 us (0.957); the launches traced: 528 us -> 497 us
  waiting for transfers between devices: 471 us -> 417 us
  blocking collectives: 0 us -> 19.5 us
    psum x1 -> x0, waiting for transfers between devices: 51.7 us -> none  [body(): grad = lax.psum(group_grad, 'rep')]
    all_gather x0 -> x1, blocking collectives: none -> 19.5 us  [body(): grad = lax.all_gather(group_grad, 'rep').sum(axis=0)]
    unnamed x4 -> x3, waiting for transfers between devices: 307 us -> 306 us
  transfers between devices with their start and end apart: 3 -> 2, of which waited for: 3 -> 2; matrix products, arithmetic and copies ran while one was open for 0% -> 1% of each run, Pallas kernels for 0% -> 0%
where the time goes in v1:
time: 506 us; the launch traced here: 497 us
  waiting for transfers between devices  417 us (82%)
  local copies, waits for them, and re-layouts  22.3 us (4%)
  blocking collectives  19.5 us (4%)
  matrix products  19.3 us (4%)
  between operations  14.1 us (3%)
    unnamed x3, waiting for transfers between devices  306 us
    all_gather x1, waiting for transfers between devices, body(): lax.all_gather(projector, 'fsdp', axis=0, tiled=True)  112 us
    unnamed x10, local copies, waits for them, and re-layouts  22.3 us
    all_gather x1, blocking collectives, body(): grad = lax.all_gather(group_grad, 'rep').sum(axis=0)  19.5 us
    dot_general x1, matrix products, body(): lax.dot_general(cotangent, low, (((0,), (0,)), ((), ())), preferred_eleme...  13.7 us
  transfers between devices with their start and end apart: 2, of which 2 were waited for; matrix products, arithmetic and copies ran while one was open for 1% of the time, Pallas kernels for 0%

profile of v1, /device:TPU:2, one launch (start us, length us, event | category | flops | bytes accessed | tf_op | source)
XLA Modules:
  0.0 496.7 jit_solution(2085593984659715943)
XLA Ops:
  7.2 0.0 copy-start
  7.2 0.0 all-gather.3.cloned.1.call-start
  7.2 0.7 all-gather.3.cloned.1.call-update
  7.9 0.0 reduce-scatter.4.cloned.1.call-start
  8.0 111.9 %all-gather.3.cloned.1.call-done = bf16[8192,256]{1,0:T(8,128)(2,1)} async-done(((bf16[128,256]{1,0:T(8,128)(2,1)}), bf16[8192,256]{1,0:T(8,128)(2,1)}) %all-gather.3.cloned.1.call-update) | async-done | bytes 4194320 | tf_op jit(solution)/shard_map/all_gather | solution.py:16
  119.8 0.0 copy-done
  119.8 13.7 %convolution_bitcast_fusion = f32[14336,256]{0,1:T(8,128)} fusion(bf16[192,14336]{1,0:T(8,128)(2,1)} %param.6, bf16[192,8192]{1,0:T(8,128)(2,1)S(1)} %copy-done, bf16[8192,256]{1,0:T(8,128)(2,1)} %all-gather.3.cloned.1.call-done), kind=kOutput, calls=%fused_computation | convolution fusion | flops 2214641664 | bytes 27525120 | tf_op jit(solution)/shard_map/dot_general | solution.py:20
  133.5 15.1 %copy.12 = f32[14336,256]{1,0:T(8,128)} copy(f32[14336,256]{0,1:T(8,128)} %convolution_bitcast_fusion) | data formatting | bytes 29360128
  148.7 0.0 copy-start.1
  148.7 0.0 reduce-scatter.4.cloned.1.call-update
  148.7 0.9 copy-done.1
  149.6 0.8 copy.8
  150.4 1.8 copy.9
  152.2 304.9 %reduce-scatter.4.cloned.1.call-done = f32[224,256]{1,0:T(8,128)} async-done(((f32[14336,256]{1,0:T(8,128)}), f32[224,256]{1,0:T(8,128)}) %reduce-scatter.4.cloned.1.call-update) | async-done | bytes 229392
  457.2 1.1 copy.13
  458.2 19.5 %all-gather = f32[1024,224]{1,0:T(8,128)} all-gather(f32[256,224]{1,0:T(8,128)S(1)} %bitcast.21), channel_id=2, replica_groups=mesh['rep'=4,'fsdp'=64] {'rep'}, dimensions={0}, use_global_device_ids=true | all-gather | bytes 1146880 | tf_op jit(solution)/shard_map/all_gather | solution.py:27
  477.8 2.0 reduce_sum.9
  479.8 1.9 fusion.1
  481.7 1.8 copy.10
  483.4 0.8 copy.11
  484.3 5.6 %fusion = bf16[8192,224]{0,1:T(8,128)(2,1)} fusion(bf16[8192,256]{1,0:T(8,128)(2,1)} %all-gather.3.cloned.1.call-done, f32[256,224]{1,0:T(8,128)S(1)} %get-tuple-element.6, f32[256,224]{1,0:T(8,128)} %get-tuple-element.7), kind=kOutput, calls=%fused_computation.2 | convolution fusion | flops 941645824 | bytes 8323072 | tf_op jit(solution)/shard_map/dot_general | solution.py:34
Async XLA Ops:
  7.2 112.7 %copy-start = (bf16[192,8192]{1,0:T(8,128)(2,1)S(1)}, bf16[192,8192]{1,0:T(8,128)(2,1)}, u32[]{:S(2)}) copy-start(bf16[192,8192]{1,0:T(8,128)(2,1)} %param.5) | copy-start | bytes 9437188
  7.2 112.6 %all-gather.3.cloned.1.call-start = ((), (), s32[]{:S(2)}) async-start(), calls=%async_computation.1 | async-start | bytes 4259840 | tf_op jit(solution)/shard_map/all_gather | solution.py:16
  7.9 449.2 %reduce-scatter.4.cloned.1.call-start = ((), (), s32[]{:S(2)}) async-start(), calls=%async_computation.2 | async-start | bytes 14909440
  148.7 0.9 copy-start.1
Sparse Core Ops, SparseCore 0:
  9.8 109.9 all-gather.2
  148.8 308.2 reduce-scatter.3

commit v2 on v0

--- a/solution.py
+++ b/solution.py
@@ -11,10 +11,14 @@
 
 
 def body(activations, cotangent, projector, moment1, moment2):
+    wait_the_patches = lambda panel, ax_name, d0: jnp.concatenate(
+        lax.all_to_all(
+            jnp.stack([panel for _ in range(lax.axis_size(ax_name))], axis=0), ax_name, 0, 0
+        ),
+        axis=d0,
+    )
     low = jnp.dot(
-        activations,
-        lax.all_gather(projector, "fsdp", axis=0, tiled=True),
-        preferred_element_type=jnp.float32,
+        activations, wait_the_patches(projector, "fsdp", d0=0), preferred_element_type=jnp.float32
     ).astype(jnp.bfloat16)
     group_grad = lax.psum_scatter(
         lax.dot_general(

time: 529 us -> 583 us (1.10)
  blocking collectives: 0 us -> 60 us
  waiting for transfers between devices: 471 us -> 461 us
    all_to_all x0 -> x1, blocking collectives: none -> 60 us  [body(): lax.all_to_all(jnp.stack([panel for _ in range(lax.axis_size(ax_name))],...]
    all_gather x1, waiting for transfers between devices: 112 us -> 103 us  [body(): lax.all_gather(projector, 'fsdp', axis=0, tiled=True)]
  transfers between devices with their start and end apart: 3 -> 3, of which waited for: 3 -> 3; matrix products, arithmetic and copies ran while one was open for 0% -> 1% of each run, Pallas kernels for 0% -> 0%
where the time goes in v2:
time: 583 us; the launch traced here: 580 us
  waiting for transfers between devices  461 us (79%)
  blocking collectives  60 us (10%)
  local copies, waits for them, and re-layouts  23.6 us (4%)
  matrix products  19.4 us (3%)
  between operations  13.8 us (2%)
    unnamed x4, waiting for transfers between devices  308 us
    all_gather x1, waiting for transfers between devices, body(): lax.all_gather(projector, 'fsdp', axis=0, tiled=True)  103 us
    all_to_all x1, blocking collectives, body(): lax.all_to_all(jnp.stack([panel for _ in range(lax.axis_size(ax_name))],...  60 us
    psum x1, waiting for transfers between devices, body(): grad = lax.psum(group_grad, 'rep')  50.8 us
    unnamed x10, local copies, waits for them, and re-layouts  22.2 us
    dot_general x1, matrix products, body(): lax.dot_general(cotangent, low, (((0,), (0,)), ((), ())), preferred_eleme...  13.7 us
  transfers between devices with their start and end apart: 3, of which 3 were waited for; matrix products, arithmetic and copies ran while one was open for 1% of the time, Pallas kernels for 0%

profile of v2, /device:TPU:2, one launch (start us, length us, event | category | flops | bytes accessed | tf_op | source)
XLA Modules:
  0.0 580.2 jit_solution(9406236051628088035)
XLA Ops:
  7.2 0.0 copy-start
  7.2 0.0 reduce-scatter.4.cloned.1.call-start
  7.2 1.5 stack.2
  8.7 60.0 %all_to_all.5 = bf16[64,128,256]{2,1,0:T(8,128)(2,1)} all-to-all(bf16[64,128,256]{2,1,0:T(8,128)(2,1)S(1)} %stack.2), channel_id=1, replica_groups=mesh['rep'=4,'fsdp'=64] {'fsdp'}, dimensions={0} | all-to-all | bytes 8388608 | tf_op jit(solution)/shard_map/all_to_all | solution.py:15
  68.7 0.0 copy-done
  68.7 13.7 %convolution_bitcast_fusion = f32[14336,256]{0,1:T(8,128)} fusion(bf16[192,14336]{1,0:T(8,128)(2,1)} %param.6, bf16[192,8192]{1,0:T(8,128)(2,1)S(1)} %copy-done, bf16[8192,256]{1,0:T(8,128)(2,1)} %bitcast.20), kind=kOutput, calls=%fused_computation | convolution fusion | flops 2214641664 | bytes 27525120 | tf_op jit(solution)/shard_map/dot_general | solution.py:24
  82.5 15.1 %copy.16 = f32[14336,256]{1,0:T(8,128)} copy(f32[14336,256]{0,1:T(8,128)} %convolution_bitcast_fusion) | data formatting | bytes 29360128
  97.6 0.0 copy-start.1
  97.6 0.0 reduce-scatter.4.cloned.1.call-update
  97.6 0.0 all-reduce.2.cloned.1.call-start
  97.7 306.8 %reduce-scatter.4.cloned.1.call-done = f32[224,256]{1,0:T(8,128)} async-done(((f32[14336,256]{1,0:T(8,128)}), f32[224,256]{1,0:T(8,128)}) %reduce-scatter.4.cloned.1.call-update) | async-done | bytes 229392
  404.5 1.8 copy.17
  406.2 0.0 all-reduce.2.cloned.1.call-update
  406.3 0.0 all-gather.2.cloned.1.call-start
  406.3 0.7 all-gather.2.cloned.1.call-update
  407.0 0.0 copy-done.1
  407.0 0.9 copy.12
  407.9 1.8 copy.13
  409.7 50.8 %all-reduce.2.cloned.1.call-done = f32[256,224]{1,0:T(8,128)} async-done(((f32[256,224]{1,0:T(8,128)}), f32[256,224]{1,0:T(8,128)}) %all-reduce.2.cloned.1.call-update) | async-done | bytes 229392 | tf_op jit(solution)/shard_map/psum | solution.py:31
  460.5 1.9 fusion.1
  462.4 1.8 copy.14
  464.2 0.8 copy.15
  465.0 103.1 %all-gather.2.cloned.1.call-done = bf16[8192,256]{1,0:T(8,128)(2,1)} async-done(((bf16[128,256]{1,0:T(8,128)(2,1)}), bf16[8192,256]{1,0:T(8,128)(2,1)}) %all-gather.2.cloned.1.call-update) | async-done | bytes 4194320 | tf_op jit(solution)/shard_map/all_gather | solution.py:39
  568.1 5.6 fusion
Async XLA Ops:
  7.2 61.6 %copy-start = (bf16[192,8192]{1,0:T(8,128)(2,1)S(1)}, bf16[192,8192]{1,0:T(8,128)(2,1)}, u32[]{:S(2)}) copy-start(bf16[192,8192]{1,0:T(8,128)(2,1)} %param.5) | copy-start | bytes 9437188
  7.2 397.3 %reduce-scatter.4.cloned.1.call-start = ((), (), s32[]{:S(2)}) async-start(), calls=%async_computation.4 | async-start | bytes 14909440
  97.6 309.4 %copy-start.1 = (f32[256,224]{0,1:T(8,128)S(1)}, f32[256,224]{0,1:T(8,128)}, u32[]{:S(2)}) copy-start(f32[256,224]{0,1:T(8,128)} %param.8) | copy-start | bytes 688132
  97.6 362.9 %all-reduce.2.cloned.1.call-start = ((), (), s32[]{:S(2)}) async-start(), calls=%async_computation.2 | async-start | bytes 524288 | tf_op jit(solution)/shard_map/psum | solution.py:31
  406.3 161.8 %all-gather.2.cloned.1.call-start = ((), (), s32[]{:S(2)}) async-start(), calls=%async_computation.3 | async-start | bytes 4259840 | tf_op jit(solution)/shard_map/all_gather | solution.py:39
Sparse Core Ops, SparseCore 0:
  97.8 306.6 reduce-scatter.3
  407.7 52.8 all-reduce.1
  462.4 105.6 all-gather.1
